TPU v7x, 128 devices: a whole 4x4x4 slice. The times are simulated.
128 devices in a mesh: dev: 128 (over x, y, z, core).
Axes of the slice: x: 4, y: 4, z: 4, core: 2. Of those that a mesh axis runs over, the one named last changes fastest.
Arguments:
- params: float32 [9, 131072], P(None, 'dev')
- moment: float32 [9, 131072], P(None, 'dev'), may hold values from -3 to 3
- second: float32 [9, 131072], P(None, 'dev'), may hold values from 0.05 to 1
- fetch_ids: int32 [128, 128, 8], P('dev'), may hold values from 0 to 1023
- seg_ids: int32 [512, 256], P('dev'), may hold values from 0 to 1023
- seg_count: int32 [512], P('dev'), may hold values from 1 to 256, 98304 in all
- seg_perm: int32 [512], replicated, may hold values from 0 to 511, as said below
- target: float32 [128, 3, 256], P('dev'), may hold values from 0 to 1
Outputs:
- image: float32 [128, 3, 256], P('dev')
- new_params: float32 [9, 131072], P(None, 'dev')
- new_moment: float32 [9, 131072], P(None, 'dev')
- new_second: float32 [9, 131072], P(None, 'dev')
Inputs may be any that keep to these rules, and one draw needn't show every extreme that they name: `seg_count`: segments that exceed their count hold unused slots; some segment is full. `seg_perm`: each number appears once.
All inputs are finite; a program needn't handle non-finite values. No bound on the sum of `seg_count` on one device may be relied on, other than what follows from the above.
Results may differ from a plain program's by a relative error of at most 0.0003.
Values sent between devices are 32-bit elements; how exact they have to be, the bound alone decides.
A program may use at most 192 MiB of HBM per device.

v0:
```python
import jax
import jax.numpy as jnp
from jax import lax
from jax.sharding import PartitionSpec as P

TILES_X = 8
KSEG = 4


def segment(par, count, tile):
    span = par.shape[1]
    pidx = jnp.arange(256, dtype=jnp.int32)
    fine_x = ((pidx % 16).astype(jnp.float32) + 0.5) / 16.0
    fine_y = ((pidx // 16).astype(jnp.float32) + 0.5) / 16.0
    pos_x = (tile % TILES_X).astype(jnp.float32) + fine_x
    pos_y = (tile // TILES_X).astype(jnp.float32) + fine_y
    steps = jnp.arange(span, dtype=jnp.int32)
    live = (steps < count).astype(jnp.float32)
    delta_x = pos_x[None, :] - par[0][:, None]
    delta_y = pos_y[None, :] - par[1][:, None]
    scale_a = jnp.exp(par[2])
    scale_c = jnp.exp(par[3])
    cross = 0.8 * jnp.tanh(par[4]) * scale_a * scale_c
    power = -0.5 * (
        (scale_a * scale_a)[:, None] * delta_x * delta_x
        + 2.0 * cross[:, None] * delta_x * delta_y
        + (scale_c * scale_c)[:, None] * delta_y * delta_y
    )
    alpha = (0.95 * jax.nn.sigmoid(par[5]) * live)[:, None] * jnp.exp(power)
    logt = jnp.log1p(-alpha)
    lower = (steps[:, None] > steps[None, :]).astype(jnp.float32)
    earlier = jnp.dot(lower, logt, precision=lax.Precision.HIGHEST)
    weight = jnp.exp(earlier) * alpha
    colour = jnp.dot(par[6:9], weight, precision=lax.Precision.HIGHEST)
    return (colour, jnp.sum(logt, axis=0))


def per_device(params, moment, second, fetch_ids, seg_ids, seg_count, seg_perm, target):
    ndev = lax.axis_size("dev")
    me = lax.axis_index("dev")
    nparam, owned = params.shape
    segs, span = seg_ids.shape
    tiles_dev = target.shape[0]
    pixels = target.shape[2]
    wanted = fetch_ids[0]
    cap = wanted.shape[1]
    received = lax.all_to_all(wanted, "dev", split_axis=0, concat_axis=0, tiled=True)
    buckets = jnp.take(params, received, axis=1)
    arrived = lax.all_to_all(buckets, "dev", split_axis=1, concat_axis=1, tiled=True)
    buffer = arrived.reshape(nparam, ndev * cap)
    first = me * segs
    own_perm = lax.dynamic_slice_in_dim(seg_perm, first, segs, 0)
    own_tile = own_perm // KSEG
    own_rank = own_perm % KSEG
    gathered_par = jnp.moveaxis(jnp.take(buffer, seg_ids, axis=1), 1, 0)

    def partials(values):
        return jax.vmap(segment)(values, seg_count, own_tile)

    (colours, logs), back = jax.vjp(partials, gathered_par)
    all_colours, all_logs, all_target = (
        lax.all_gather(colours, "dev", axis=0, tiled=True),
        lax.all_gather(logs, "dev", axis=0, tiled=True),
        lax.all_gather(target, "dev", axis=0, tiled=True),
    )
    total = all_logs.shape[0]
    ntiles = all_target.shape[0]
    tile_all = seg_perm // KSEG
    rank_all = seg_perm % KSEG
    same = tile_all[:, None] == tile_all[None, :]
    before = (same & (rank_all[None, :] < rank_all[:, None])).astype(jnp.float32)
    prefix = jnp.exp(jnp.dot(before, all_logs, precision=lax.Precision.HIGHEST))
    contrib = (prefix[:, None, :] * all_colours).reshape(total, 3 * pixels)
    onehot = (jnp.arange(ntiles, dtype=jnp.int32)[:, None] == tile_all[None, :]).astype(jnp.float32)
    image = jnp.dot(onehot, contrib, precision=lax.Precision.HIGHEST)
    misfit = image - all_target.reshape(ntiles, 3 * pixels)
    later = (
        (own_tile[:, None] == tile_all[None, :]) & (rank_all[None, :] > own_rank[:, None])
    ).astype(jnp.float32)
    behind = jnp.dot(later, contrib, precision=lax.Precision.HIGHEST).reshape(segs, 3, pixels)
    picker = (own_tile[:, None] == jnp.arange(ntiles, dtype=jnp.int32)[None, :]).astype(jnp.float32)
    error = jnp.dot(picker, misfit, precision=lax.Precision.HIGHEST).reshape(segs, 3, pixels)
    own_prefix = lax.dynamic_slice_in_dim(prefix, first, segs, 0)
    d_colour = own_prefix[:, None, :] * error
    d_log = jnp.sum(error * behind, axis=1)
    (d_par,) = back((d_colour, d_log))
    slot_grad = (
        jnp.zeros((nparam, ndev * cap), jnp.float32)
        .at[:, seg_ids.reshape(-1)]
        .add(jnp.moveaxis(d_par, 1, 0).reshape(nparam, segs * span))
    )
    returned = lax.all_to_all(
        slot_grad.reshape(nparam, ndev, cap), "dev", split_axis=1, concat_axis=1, tiled=True
    )
    grad = (
        jnp.zeros((nparam, owned), jnp.float32)
        .at[:, received.reshape(-1)]
        .add(returned.reshape(nparam, ndev * cap))
    )
    new_moment = 0.9 * moment + 0.1 * grad
    new_second = 0.99 * second + 0.01 * grad * grad
    new_params = params - 0.05 * new_moment / (jnp.sqrt(new_second) + 1e-08)
    my_image = lax.dynamic_slice_in_dim(image, me * tiles_dev, tiles_dev, 0).reshape(
        tiles_dev, 3, pixels
    )
    return (my_image, new_params, new_moment, new_second)


def solution(mesh):
    placed = (
        P(None, "dev"),
        P(None, "dev"),
        P(None, "dev"),
        P("dev", None, None),
        P("dev", None),
        P("dev"),
        P(),
        P("dev", None, None),
    )
    return jax.shard_map(
        per_device,
        mesh=mesh,
        in_specs=placed,
        out_specs=(P("dev", None, None), P(None, "dev"), P(None, "dev"), P(None, "dev")),
        check_vma=False,
    )
```

profile of v0, /device:TPU:1, one launch (start us, length us, event | category | flops | bytes accessed | tf_op | source)
XLA Modules:
  0.0 180.8 jit_solution(5734400977405865448)
XLA Ops:
  7.2 1.4 copy.73
  8.6 11.5 %all-to-all-start = ((s32[128,1,8]{2,1,0:T(1,128)}), s32[128,1,8]{2,1,0:T(1,128)S(1)}, u32[]{:S(2)}, u32[]{:S(2)}) async-start(s32[128,1,8]{2,1,0:T(1,128)} %bitcast), calls=%async_computation | async-start | bytes 131072 | tf_op jit(solution)/shard_map/all_to_all | solution.py:47
  20.1 0.7 fusion.92
  20.8 0.7 compare_and_fusion.1
  21.5 0.8 and_select_fusion
  22.3 0.8 fusion.102
  23.0 0.1 broadcast_add_fusion.1
  23.1 1.1 copy.74
  24.2 5.2 %all-to-all-done = s32[128,1,8]{2,1,0:T(1,128)S(1)} async-done(((s32[128,1,8]{2,1,0:T(1,128)}), s32[128,1,8]{2,1,0:T(1,128)S(1)}, u32[]{:S(2)}, u32[]{:S(2)}) %all-to-all-start) | async-done | bytes 4128 | tf_op jit(solution)/shard_map/all_to_all | solution.py:47
  29.4 0.1 reshape.400
  29.5 2.8 %gather_fusion = f32[1024,9]{1,0:T(8,128)S(1)} fusion(f32[9,1024]{0,1:T(8,128)S(1)} %copy.74, s32[1024]{0:T(1024)S(1)} %broadcast_clamp_fusion.1), kind=kCustom, calls=%fused_computation | custom fusion | bytes 77824 | tf_op jit(solution)/shard_map/jit(_take)/gather | solution.py:48
  32.3 0.0 copy-start.6
  32.4 1.0 fusion.43
  33.4 4.8 %all-to-all-start.1 = ((f32[9,128,8]{0,2,1:T(8,128)}), f32[9,128,8]{0,2,1:T(8,128)S(1)}, u32[]{:S(2)}, u32[]{:S(2)}) async-start(f32[9,128,8]{0,2,1:T(8,128)} %fusion.43), calls=%async_computation.1 | async-start | bytes 1048576 | tf_op jit(solution)/shard_map/all_to_all | solution.py:49
  38.1 0.0 all-gather.3.cloned.1.call-start
  38.2 13.5 %all-to-all-done.1 = f32[9,128,8]{0,2,1:T(8,128)S(1)} async-done(((f32[9,128,8]{0,2,1:T(8,128)}), f32[9,128,8]{0,2,1:T(8,128)S(1)}, u32[]{:S(2)}, u32[]{:S(2)}) %all-to-all-start.1) | async-done | bytes 36896 | tf_op jit(solution)/shard_map/all_to_all | solution.py:49
  51.7 2.8 %gather_fusion.1 = f32[1024,9]{1,0:T(8,128)S(1)} fusion(f32[9,1024]{0,1:T(8,128)S(1)} %bitcast.116, s32[1024]{0:T(1024)S(1)} %broadcast_clamp_fusion), kind=kCustom, calls=%fused_computation.1 | custom fusion | bytes 77824 | tf_op jit(solution)/shard_map/jit(_take)/gather | solution.py:55
  54.5 0.2 copy.76
  54.8 0.0 copy-done.6
  54.8 0.1 bitcast_select_fusion.1
  54.9 1.5 convolution_exponential_fusion
  56.3 0.0 copy-start.7
  56.3 0.0 copy-start.3
  56.4 0.0 copy-start.5
  56.4 2.1 %fusion.60 = f32[4,3,256]{2,1,0:T(4,128)} fusion(f32[256,4,256]{0,2,1:T(8,128)S(1)} %convolution_exponential_fusion, f32[4,256]{1,0:T(4,128)S(1)} %get-tuple-element.48, f32[4,256]{1,0:T(4,128)S(1)} %get-tuple-element.51, f32[4,256]{1,0:T(4,128)S(1)} %get-tuple-element.56, f32[4,256]{1,0:T(4,128)S(1)} %get-tuple-element.44, ...), kind=kOutput, calls=%fused_computation.86 | convolution fusion | flops 12845056 | bytes 1110016 | tf_op jit(solution)/shard_map/jvp(vmap())/dot_general | solution.py:34
  58.5 0.0 copy-done.7
  58.5 0.0 all-gather.3.cloned.1.call-update
  58.5 0.0 copy-done.3
  58.5 33.7 %all_gather.11 = f32[128,3,256]{2,1,0:T(4,128)S(1)} all-gather(f32[1,3,256]{2,1,0:T(4,128)S(1)} %copy.80), channel_id=1, replica_groups=mesh['dev'=128] {'dev'}, dimensions={0}, use_global_device_ids=true | all-gather | bytes 396288 | tf_op jit(solution)/shard_map/all_gather | solution.py:64
  92.3 0.2 copy.81
  92.5 0.2 copy.82
  92.7 0.0 copy-done.4
  92.7 0.5 broadcast.499
  93.2 0.8 reduce.3
  94.0 0.1 reshape.387
  94.1 1.0 log-plus-one_reduce_fusion
  95.2 35.5 %all-gather = f32[128,4,256]{2,1,0:T(4,128)S(1)} all-gather(f32[1,4,256]{2,1,0:T(4,128)S(1)} %bitcast.127), channel_id=1, replica_groups=mesh['dev'=128] {'dev'}, dimensions={0}, use_global_device_ids=true | all-gather | bytes 528384 | tf_op jit(solution)/shard_map/all_gather | solution.py:63
  130.7 0.2 reshape.434
  130.9 0.7 convolution_exponential_fusion.1
  131.6 0.2 copy.77
  131.8 0.0 all-gather.3.cloned.1.call-done
  131.9 1.8 %copy.79 = f32[512,3,256]{0,2,1:T(8,128)S(1)} copy(f32[512,3,256]{2,1,0:T(4,128)} %all-gather.3.cloned.1.call-done) | data formatting | bytes 3145728 | tf_op jit(solution)/shard_map/all_gather | solution.py:62
  133.7 0.2 broadcast_multiply_fusion
  133.9 1.0 fusion.66
  134.9 0.3 fusion.61
  135.2 1.1 fusion.72
  136.3 0.0 copy-done.8
  136.3 1.2 fusion.59
  137.5 0.8 fusion.12
  138.3 3.0 %fusion.33 = (f32[4,256]{1,0:T(4,128)S(1)}, f32[4,256]{1,0:T(4,128)S(1)}, f32[4,256]{1,0:T(4,128)S(1)}, f32[4,256]{1,0:T(4,128)S(1)}, f32[4,256]{1,0:T(4,128)S(1)}, /*index=5*/f32[4,256]{1,0:T(4,128)S(1)}) fusion(f32[4,256]{1,0:T(4,128)S(1)} %get-tuple-element.51, f32[4,256]{1,0:T(4,128)S(1)} %get-tuple-element.56, f32[4,256]{1,0:T(4,128)S(1)} %get-tuple-element.48, ...), kind=kOutput, calls=%fused_computation.52 | convolution fusion | flops 820570112 | bytes 2183168 | tf_op jit(solution)/shard_map/transpose(jvp(vmap()))/dot_general | solution.py:32
  141.4 0.1 fusion.81
  141.5 0.1 add_bitcast_fusion
  141.7 0.2 copy.87
  141.9 0.0 copy-start
  141.9 0.0 copy-start.1
  141.9 0.0 copy-start.2
  141.9 6.8 %scatter_custom_fusion = f32[9,1024]{0,1:T(8,128)} fusion(s32[1024]{0:T(1024)S(1)} %bitcast.130, f32[1024,9]{1,0:T(8,128)S(1)} %copy.87, f32[]{:T(128)} %constant.149.clone.1), kind=kCustom, calls=%fused_computation.90 | custom fusion | flops 9216 | bytes 36868 | tf_op jit(solution)/shard_map/scatter-add | solution.py:90
  148.7 4.6 %all-to-all-start.2 = ((f32[9,128,8]{0,2,1:T(8,128)}), f32[9,128,8]{0,2,1:T(8,128)S(1)}, u32[]{:S(2)}, u32[]{:S(2)}) async-start(f32[9,128,8]{0,2,1:T(8,128)} %bitcast.30), calls=%async_computation.2 | async-start | bytes 1048576 | tf_op jit(solution)/shard_map/all_to_all | solution.py:92
  153.4 0.6 constant_dynamic-slice_fusion.1
  154.0 13.0 %all-to-all-done.2 = f32[9,128,8]{0,2,1:T(8,128)S(1)} async-done(((f32[9,128,8]{0,2,1:T(8,128)}), f32[9,128,8]{0,2,1:T(8,128)S(1)}, u32[]{:S(2)}, u32[]{:S(2)}) %all-to-all-start.2) | async-done | bytes 36896 | tf_op jit(solution)/shard_map/all_to_all | solution.py:92
  166.9 6.2 %scatter_custom_fusion.1 = f32[9,1024]{0,1:T(8,128)S(1)} fusion(s32[1024]{0:T(1024)S(1)} %bitcast.129, f32[9,128,8]{0,2,1:T(8,128)S(1)} %all-to-all-done.2, f32[]{:T(128)} %constant.149.clone.1), kind=kCustom, calls=%fused_computation.67 | custom fusion | flops 9216 | bytes 561156 | tf_op jit(solution)/shard_map/scatter-add | solution.py:98
  173.1 0.2 copy.88
  173.3 0.0 copy-done.2
  173.3 0.7 divide_subtract_fusion
  (34 shorter events, 0.3 us)
Async XLA Ops:
  8.6 20.8 %all-to-all-start = ((s32[128,1,8]{2,1,0:T(1,128)}), s32[128,1,8]{2,1,0:T(1,128)S(1)}, u32[]{:S(2)}, u32[]{:S(2)}) async-start(s32[128,1,8]{2,1,0:T(1,128)} %bitcast), calls=%async_computation | async-start | bytes 131072 | tf_op jit(solution)/shard_map/all_to_all | solution.py:47
  32.3 22.4 %copy-start.6 = (s32[4]{0:T(128)S(1)}, s32[4]{0:T(128)}, u32[]{:S(2)}) copy-start(s32[4]{0:T(128)} %param.13) | copy-start | bytes 52
  33.4 18.3 %all-to-all-start.1 = ((f32[9,128,8]{0,2,1:T(8,128)}), f32[9,128,8]{0,2,1:T(8,128)S(1)}, u32[]{:S(2)}, u32[]{:S(2)}) async-start(f32[9,128,8]{0,2,1:T(8,128)} %fusion.43), calls=%async_computation.1 | async-start | bytes 1048576 | tf_op jit(solution)/shard_map/all_to_all | solution.py:49
  38.1 93.7 %all-gather.3.cloned.1.call-start = ((), (), s32[]{:S(2)}) async-start(), calls=%async_computation.3 | async-start | bytes 2113536 | tf_op jit(solution)/shard_map/all_gather | solution.py:62
  56.3 2.1 %copy-start.7 = (f32[256,4,256]{0,2,1:T(8,128)}, f32[256,4,256]{0,2,1:T(8,128)S(1)}, u32[]{:S(2)}) copy-start(f32[256,4,256]{0,2,1:T(8,128)S(1)} %convolution_exponential_fusion) | copy-start | bytes 3145732
  56.3 2.2 %copy-start.3 = (s32[4,256]{1,0:T(4,128)S(1)}, s32[4,256]{1,0:T(4,128)}, u32[]{:S(2)}) copy-start(s32[4,256]{1,0:T(4,128)} %param.12) | copy-start | bytes 12292
  56.4 2.2 %copy-start.5 = (f32[1,3,256]{2,0,1:T(1,128)S(1)}, f32[1,3,256]{2,0,1:T(1,128)}, u32[]{:S(2)}) copy-start(f32[1,3,256]{2,0,1:T(1,128)} %param.15) | copy-start | bytes 9220
  58.5 34.2 %copy-start.4 = (s32[512]{0:T(512)S(1)}, s32[512]{0:T(512)}, u32[]{:S(2)}) copy-start(s32[512]{0:T(512)} %param.14) | copy-start | bytes 6148
  133.9 2.4 %copy-start.8 = (f32[256,4,256]{0,2,1:T(8,128)S(1)}, f32[256,4,256]{0,2,1:T(8,128)}, u32[]{:S(2)}) copy-start(f32[256,4,256]{0,2,1:T(8,128)} %copy-done.7) | copy-start | bytes 3145732
  141.9 31.4 %copy-start = (f32[9,1024]{1,0:T(8,128)S(1)}, f32[9,1024]{1,0:T(8,128)}, u32[]{:S(2)}) copy-start(f32[9,1024]{1,0:T(8,128)} %param.8) | copy-start | bytes 110596
  141.9 31.4 %copy-start.1 = (f32[9,1024]{1,0:T(8,128)S(1)}, f32[9,1024]{1,0:T(8,128)}, u32[]{:S(2)}) copy-start(f32[9,1024]{1,0:T(8,128)} %param.9) | copy-start | bytes 110596
  141.9 31.4 %copy-start.2 = (f32[9,1024]{1,0:T(8,128)S(1)}, f32[9,1024]{1,0:T(8,128)}, u32[]{:S(2)}) copy-start(f32[9,1024]{1,0:T(8,128)} %param.10) | copy-start | bytes 110596
  148.7 18.2 %all-to-all-start.2 = ((f32[9,128,8]{0,2,1:T(8,128)}), f32[9,128,8]{0,2,1:T(8,128)S(1)}, u32[]{:S(2)}, u32[]{:S(2)}) async-start(f32[9,128,8]{0,2,1:T(8,128)} %bitcast.30), calls=%async_computation.2 | async-start | bytes 1048576 | tf_op jit(solution)/shard_map/all_to_all | solution.py:92
Sparse Core Ops, SparseCore 0:
  58.6 62.3 all-gather.2
where the time goes:
time: 181 us
  blocking collectives  69.2 us (38%)
  waiting for transfers between devices  31.7 us (18%)
  starting transfers between devices  20.9 us (12%)
  other arithmetic  20.1 us (11%)
  between operations  14.5 us (8%)
  local copies, waits for them, and re-layouts  12.7 us (7%)
  matrix products  11.7 us (6%)
    all_gather x1, blocking collectives, per_device(): lax.all_gather(logs, 'dev', axis=0, tiled=True)  35.5 us
    all_gather x1, blocking collectives, per_device(): lax.all_gather(target, 'dev', axis=0, tiled=True)  33.7 us
    all_to_all x1, waiting for transfers between devices, per_device(): lax.all_to_all(buckets, 'dev', split_axis=1, concat_axis=1, tiled=True)  13.5 us
    all_to_all x1, waiting for transfers between devices, per_device(): lax.all_to_all(slot_grad.reshape(nparam, ndev, cap), 'dev', split_axis=1,...  13 us
    all_to_all x1, starting transfers between devices, per_device(): lax.all_to_all(wanted, 'dev', split_axis=0, concat_axis=0, tiled=True)  11.5 us
    scatter-add x1, other arithmetic, per_device(): slot_grad = jnp.zeros((nparam, ndev * cap), jnp.float32).at[:, seg_ids.re...  6.79 us
    scatter-add x1, other arithmetic, per_device(): grad = jnp.zeros((nparam, owned), jnp.float32).at[:, received.reshape(-1)...  6.18 us
    all_to_all x1, waiting for transfers between devices, per_device(): lax.all_to_all(wanted, 'dev', split_axis=0, concat_axis=0, tiled=True)  5.21 us
  transfers between devices with their start and end apart: 4, of which 3 were waited for; matrix products, arithmetic and copies ran while one was open for 5% of the time, Pallas kernels for 0%

commit v1 on v0

--- a/solution.py
+++ b/solution.py
@@ -46,7 +46,15 @@
     cap = wanted.shape[1]
     received = lax.all_to_all(wanted, "dev", split_axis=0, concat_axis=0, tiled=True)
     buckets = jnp.take(params, received, axis=1)
-    arrived = lax.all_to_all(buckets, "dev", split_axis=1, concat_axis=1, tiled=True)
+    arrived = jnp.concatenate(
+        lax.all_to_all(
+            jnp.stack(jnp.split(buckets, lax.axis_size("dev"), 1), 0),
+            split_axis=0,
+            axis_name="dev",
+            concat_axis=0,
+        ),
+        axis=1,
+    )
     buffer = arrived.reshape(nparam, ndev * cap)
     first = me * segs
     own_perm = lax.dynamic_slice_in_dim(seg_perm, first, segs, 0)

time: 181 us -> 256 us (1.41)
  local copies, waits for them, and re-layouts: 12.7 us -> 88.3 us
    unnamed x27 -> x154, local copies, waits for them, and re-layouts: 2.74 us -> 77.7 us
  transfers between devices with their start and end apart: 4 -> 4, of which waited for: 3 -> 3; matrix products, arithmetic and copies ran while one was open for 5% -> 3% of each run, Pallas kernels for 0% -> 0%
where the time goes in v1:
time: 256 us
  local copies, waits for them, and re-layouts  88.3 us (34%)
  blocking collectives  69.2 us (27%)
  waiting for transfers between devices  31.7 us (12%)
  starting transfers between devices  20.9 us (8%)
  other arithmetic  19.3 us (8%)
  between operations  14.6 us (6%)
  matrix products  11.7 us (5%)
    unnamed x154, local copies, waits for them, and re-layouts  77.7 us
    all_gather x1, blocking collectives, per_device(): lax.all_gather(logs, 'dev', axis=0, tiled=True)  35.5 us
    all_gather x1, blocking collectives, per_device(): lax.all_gather(target, 'dev', axis=0, tiled=True)  33.7 us
    all_to_all x1, waiting for transfers between devices, per_device(): lax.all_to_all(jnp.stack(jnp.split(buckets, lax.axis_size('dev'), 1), 0),...  13.5 us
    all_to_all x1, waiting for transfers between devices, per_device(): lax.all_to_all(slot_grad.reshape(nparam, ndev, cap), 'dev', split_axis=1,...  13 us
    all_to_all x1, starting transfers between devices, per_device(): lax.all_to_all(wanted, 'dev', split_axis=0, concat_axis=0, tiled=True)  11.5 us
    scatter-add x1, other arithmetic, per_device(): slot_grad = jnp.zeros((nparam, ndev * cap), jnp.float32).at[:, seg_ids.re...  6.79 us
    scatter-add x1, other arithmetic, per_device(): grad = jnp.zeros((nparam, owned), jnp.float32).at[:, received.reshape(-1)...  6.18 us
  transfers between devices with their start and end apart: 4, of which 3 were waited for; matrix products, arithmetic and copies ran while one was open for 3% of the time, Pallas kernels for 0%

profile of v1, /device:TPU:1, one launch (start us, length us, event | category | flops | bytes accessed | tf_op | source)
XLA Modules:
  0.0 255.7 jit_solution(10693653764617691195)
XLA Ops:
  7.2 1.4 copy.530
  8.6 11.5 %all-to-all-start = ((s32[128,1,8]{2,1,0:T(1,128)}), s32[128,1,8]{2,1,0:T(1,128)S(1)}, u32[]{:S(2)}, u32[]{:S(2)}) async-start(s32[128,1,8]{2,1,0:T(1,128)} %bitcast), calls=%async_computation | async-start | bytes 131072 | tf_op jit(solution)/shard_map/all_to_all | solution.py:47
  20.1 0.7 fusion.92
  20.8 0.7 compare_and_fusion.1
  21.5 0.8 and_select_fusion
  22.3 0.8 fusion.102
  23.1 1.1 copy.531
  24.2 5.2 %all-to-all-done = s32[128,1,8]{2,1,0:T(1,128)S(1)} async-done(((s32[128,1,8]{2,1,0:T(1,128)}), s32[128,1,8]{2,1,0:T(1,128)S(1)}, u32[]{:S(2)}, u32[]{:S(2)}) %all-to-all-start) | async-done | bytes 4128 | tf_op jit(solution)/shard_map/all_to_all | solution.py:47
  29.5 2.8 %gather_fusion = f32[1024,9]{1,0:T(8,128)S(1)} fusion(f32[9,1024]{0,1:T(8,128)S(1)} %copy.531, s32[1024]{0:T(1024)S(1)} %broadcast_clamp_fusion.1), kind=kCustom, calls=%fused_computation | custom fusion | bytes 77824 | tf_op jit(solution)/shard_map/jit(_take)/gather | solution.py:48
  32.6 0.6 constant_dynamic-update-slice_fusion.127
  33.2 0.6 constant_dynamic-update-slice_fusion.126
  36.1 0.6 constant_dynamic-update-slice_fusion.121
  38.5 0.6 constant_dynamic-update-slice_fusion.117
  40.2 0.6 constant_dynamic-update-slice_fusion.114
  43.2 0.6 constant_dynamic-update-slice_fusion.109
  43.8 0.6 constant_dynamic-update-slice_fusion.108
  45.0 0.6 constant_dynamic-update-slice_fusion.106
  46.7 0.6 constant_dynamic-update-slice_fusion.103
  47.9 0.6 constant_dynamic-update-slice_fusion.101
  49.1 0.6 constant_dynamic-update-slice_fusion.99
  53.8 0.6 constant_dynamic-update-slice_fusion.91
  56.8 0.6 constant_dynamic-update-slice_fusion.86
  59.8 0.6 constant_dynamic-update-slice_fusion.81
  60.4 0.6 constant_dynamic-update-slice_fusion.80
  62.7 0.6 constant_dynamic-update-slice_fusion.76
  63.9 0.6 constant_dynamic-update-slice_fusion.74
  66.3 0.6 constant_dynamic-update-slice_fusion.70
  69.2 0.6 constant_dynamic-update-slice_fusion.65
  72.8 0.6 constant_dynamic-update-slice_fusion.59
  75.1 0.6 constant_dynamic-update-slice_fusion.55
  78.7 0.6 constant_dynamic-update-slice_fusion.49
  79.3 0.6 constant_dynamic-update-slice_fusion.48
  81.1 0.6 constant_dynamic-update-slice_fusion.45
  81.7 0.6 constant_dynamic-update-slice_fusion.44
  82.8 0.6 constant_dynamic-update-slice_fusion.42
  87.6 0.6 constant_dynamic-update-slice_fusion.34
  89.9 0.6 constant_dynamic-update-slice_fusion.30
  91.1 0.6 constant_dynamic-update-slice_fusion.28
  95.8 0.6 constant_dynamic-update-slice_fusion.20
  96.4 0.6 constant_dynamic-update-slice_fusion.19
  100.0 0.6 constant_dynamic-update-slice_fusion.13
  100.6 0.6 constant_dynamic-update-slice_fusion.12
  107.6 0.6 constant_dynamic-update-slice_fusion
  108.2 4.8 %all-to-all-start.1 = ((f32[128,9,1,8]{1,3,2,0:T(8,128)}), f32[128,9,1,8]{1,3,2,0:T(8,128)S(1)}, u32[]{:S(2)}, u32[]{:S(2)}) async-start(f32[128,9,1,8]{1,3,2,0:T(8,128)} %constant_dynamic-update-slice_fusion), calls=%async_computation.1 | async-start | bytes 1048576 | tf_op jit(solution)/shard_map/all_to_all | solution.py:50
  113.0 13.5 %all-to-all-done.1 = f32[128,9,1,8]{1,3,2,0:T(8,128)S(1)} async-done(((f32[128,9,1,8]{1,3,2,0:T(8,128)}), f32[128,9,1,8]{1,3,2,0:T(8,128)S(1)}, u32[]{:S(2)}, u32[]{:S(2)}) %all-to-all-start.1) | async-done | bytes 36896 | tf_op jit(solution)/shard_map/all_to_all | solution.py:50
  126.5 2.8 %gather_fusion.1 = f32[1024,9]{1,0:T(8,128)S(1)} fusion(f32[9,1024]{0,1:T(8,128)S(1)} %bitcast.630, s32[1024]{0:T(1024)S(1)} %broadcast_clamp_fusion), kind=kCustom, calls=%fused_computation.1 | custom fusion | bytes 77824 | tf_op jit(solution)/shard_map/jit(_take)/gather | solution.py:63
  129.7 1.5 convolution_exponential_fusion
  131.2 2.1 fusion.60
  133.4 33.7 %all_gather.11 = f32[128,3,256]{2,1,0:T(4,128)S(1)} all-gather(f32[1,3,256]{2,1,0:T(4,128)S(1)} %copy.537), channel_id=1, replica_groups=mesh['dev'=128] {'dev'}, dimensions={0}, use_global_device_ids=true | all-gather | bytes 396288 | tf_op jit(solution)/shard_map/all_gather | solution.py:72
  168.1 0.8 reduce.3
  169.0 1.0 log-plus-one_reduce_fusion
  170.0 35.5 %all-gather = f32[128,4,256]{2,1,0:T(4,128)S(1)} all-gather(f32[1,4,256]{2,1,0:T(4,128)S(1)} %bitcast.641), channel_id=1, replica_groups=mesh['dev'=128] {'dev'}, dimensions={0}, use_global_device_ids=true | all-gather | bytes 528384 | tf_op jit(solution)/shard_map/all_gather | solution.py:71
  205.7 0.7 convolution_exponential_fusion.1
  206.7 1.8 copy.536
  208.8 1.0 fusion.66
  210.1 1.1 fusion.72
  211.2 1.2 fusion.59
  212.3 0.8 fusion.12
  213.2 3.0 %fusion.33 = (f32[4,256]{1,0:T(4,128)S(1)}, f32[4,256]{1,0:T(4,128)S(1)}, f32[4,256]{1,0:T(4,128)S(1)}, f32[4,256]{1,0:T(4,128)S(1)}, f32[4,256]{1,0:T(4,128)S(1)}, /*index=5*/f32[4,256]{1,0:T(4,128)S(1)}) fusion(f32[4,256]{1,0:T(4,128)S(1)} %get-tuple-element.63, f32[4,256]{1,0:T(4,128)S(1)} %get-tuple-element.68, f32[4,256]{1,0:T(4,128)S(1)} %get-tuple-element.60, ...), kind=kOutput, calls=%fused_computation.52 | convolution fusion | flops 820570112 | bytes 2183168 | tf_op jit(solution)/shard_map/transpose(jvp(vmap()))/dot_general | solution.py:32
  216.8 6.8 %scatter_custom_fusion = f32[9,1024]{0,1:T(8,128)} fusion(s32[1024]{0:T(1024)S(1)} %bitcast.644, f32[1024,9]{1,0:T(8,128)S(1)} %copy.544, f32[]{:T(128)} %constant.149.clone.1), kind=kCustom, calls=%fused_computation.218 | custom fusion | flops 9216 | bytes 36868 | tf_op jit(solution)/shard_map/scatter-add | solution.py:98
  223.6 4.6 %all-to-all-start.2 = ((f32[9,128,8]{0,2,1:T(8,128)}), f32[9,128,8]{0,2,1:T(8,128)S(1)}, u32[]{:S(2)}, u32[]{:S(2)}) async-start(f32[9,128,8]{0,2,1:T(8,128)} %bitcast.159), calls=%async_computation.2 | async-start | bytes 1048576 | tf_op jit(solution)/shard_map/all_to_all | solution.py:100
  228.8 13.0 %all-to-all-done.2 = f32[9,128,8]{0,2,1:T(8,128)S(1)} async-done(((f32[9,128,8]{0,2,1:T(8,128)}), f32[9,128,8]{0,2,1:T(8,128)S(1)}, u32[]{:S(2)}, u32[]{:S(2)}) %all-to-all-start.2) | async-done | bytes 36896 | tf_op jit(solution)/shard_map/all_to_all | solution.py:100
  241.8 6.2 %scatter_custom_fusion.1 = f32[9,1024]{0,1:T(8,128)S(1)} fusion(s32[1024]{0:T(1024)S(1)} %bitcast.643, f32[9,128,8]{0,2,1:T(8,128)S(1)} %all-to-all-done.2, f32[]{:T(128)} %constant.149.clone.1), kind=kCustom, calls=%fused_computation.67 | custom fusion | flops 9216 | bytes 561156 | tf_op jit(solution)/shard_map/scatter-add | solution.py:106
  248.2 0.7 divide_subtract_fusion
  (162 shorter events, 59.4 us)
Async XLA Ops:
  8.6 20.8 %all-to-all-start = ((s32[128,1,8]{2,1,0:T(1,128)}), s32[128,1,8]{2,1,0:T(1,128)S(1)}, u32[]{:S(2)}, u32[]{:S(2)}) async-start(s32[128,1,8]{2,1,0:T(1,128)} %bitcast), calls=%async_computation | async-start | bytes 131072 | tf_op jit(solution)/shard_map/all_to_all | solution.py:47
  42.6 87.0 %copy-start.6 = (s32[4]{0:T(128)S(1)}, s32[4]{0:T(128)}, u32[]{:S(2)}) copy-start(s32[4]{0:T(128)} %param.13) | copy-start | bytes 52
  108.2 18.3 %all-to-all-start.1 = ((f32[128,9,1,8]{1,3,2,0:T(8,128)}), f32[128,9,1,8]{1,3,2,0:T(8,128)S(1)}, u32[]{:S(2)}, u32[]{:S(2)}) async-start(f32[128,9,1,8]{1,3,2,0:T(8,128)} %constant_dynamic-update-slice_fusion), calls=%async_computation.1 | async-start | bytes 1048576 | tf_op jit(solution)/shard_map/all_to_all | solution.py:50
  113.0 93.7 %all-gather.3.cloned.1.call-start = ((), (), s32[]{:S(2)}) async-start(), calls=%async_computation.3 | async-start | bytes 2113536 | tf_op jit(solution)/shard_map/all_gather | solution.py:70
  131.2 2.1 copy-start.7
  131.2 2.2 copy-start.3
  131.2 2.2 copy-start.5
  133.3 34.2 %copy-start.4 = (s32[512]{0:T(512)S(1)}, s32[512]{0:T(512)}, u32[]{:S(2)}) copy-start(s32[512]{0:T(512)} %param.14) | copy-start | bytes 6148
  208.8 2.4 copy-start.8
  216.8 31.4 %copy-start = (f32[9,1024]{1,0:T(8,128)S(1)}, f32[9,1024]{1,0:T(8,128)}, u32[]{:S(2)}) copy-start(f32[9,1024]{1,0:T(8,128)} %param.8) | copy-start | bytes 110596
  216.8 31.4 %copy-start.1 = (f32[9,1024]{1,0:T(8,128)S(1)}, f32[9,1024]{1,0:T(8,128)}, u32[]{:S(2)}) copy-start(f32[9,1024]{1,0:T(8,128)} %param.9) | copy-start | bytes 110596
  216.8 31.4 %copy-start.2 = (f32[9,1024]{1,0:T(8,128)S(1)}, f32[9,1024]{1,0:T(8,128)}, u32[]{:S(2)}) copy-start(f32[9,1024]{1,0:T(8,128)} %param.10) | copy-start | bytes 110596
  223.6 18.2 %all-to-all-start.2 = ((f32[9,128,8]{0,2,1:T(8,128)}), f32[9,128,8]{0,2,1:T(8,128)S(1)}, u32[]{:S(2)}, u32[]{:S(2)}) async-start(f32[9,128,8]{0,2,1:T(8,128)} %bitcast.159), calls=%async_computation.2 | async-start | bytes 1048576 | tf_op jit(solution)/shard_map/all_to_all | solution.py:100
Sparse Core Ops, SparseCore 0:
  133.5 62.3 all-gather.2
